TPU v7x, 256 devices: a whole 4x4x8 slice. The times are simulated.
256 devices in a mesh: dp: 32 (over y, z_lo, core), cent: 8 (over x, z_hi).
Axes of the slice: x: 4, y: 4, z: 8 (z_hi: 2, z_lo: 4; z = z_hi * 4 + z_lo), core: 2. Of those that a mesh axis runs over, the one named last changes fastest.
Arguments:
- hidden: bfloat16 [5632, 11008], P('dp', 'cent'), may hold values from -6 to 6
- residual: bfloat16 [5632, 4096], P('dp', 'cent'), may hold values from -6 to 6
- down_weight: bfloat16 [11008, 4096], P('cent', 'dp'), may hold values from -0.0546875 to 0.0546875
- gain: float32 [4096], P('cent'), may hold values from 0.1 to 1.9
- proj_weight: bfloat16 [4096, 1024], P('cent'), may hold values from -0.09375 to 0.09375
- centroids: bfloat16 [131072, 1024], P(('dp', 'cent')), may hold values from -24 to 24
Outputs:
- weighted: float32 [131072, 1024], P(('dp', 'cent'))
- counts: float32 [131072], P(('dp', 'cent'))
All inputs are finite; a program needn't handle non-finite values.
Results may differ from a plain program's by a relative error of at most 0.011.
Values may be sent and summed in bfloat16 or wider, within the bound.
A program may use at most 128 MiB of HBM per device.

v0:
```python
import math
import jax
import jax.numpy as jnp
from jax import lax
from jax.sharding import PartitionSpec as P


def body(hidden, residual, down_weight, gain, proj_weight, centroids):
    partial_layer = jnp.dot(
        hidden,
        lax.all_gather(down_weight, "dp", axis=1, tiled=True),
        preferred_element_type=jnp.float32,
    )
    layer_out = lax.psum_scatter(partial_layer, "cent", scatter_dimension=1, tiled=True)
    normed = ((layer_out + residual.astype(jnp.float32)) * gain).astype(jnp.bfloat16)
    partial_embed = jnp.dot(normed, proj_weight, preferred_element_type=jnp.float32)
    embed_width = proj_weight.shape[1]
    embed_full = lax.psum(partial_embed, "cent")
    scaled = (
        embed_full * lax.rsqrt(jnp.mean(embed_full * embed_full, axis=1, keepdims=True) + 1e-06)
    ).astype(jnp.bfloat16)
    gathered = lax.all_gather(scaled, "dp", axis=0, tiled=True)
    inverse = 1.0 / (math.sqrt(embed_width) * 0.05)
    scores = (
        lax.dot_general(
            gathered, centroids, (((1,), (1,)), ((), ())), preferred_element_type=jnp.float32
        )
        * inverse
    )
    local_max = jnp.max(scores, axis=1)
    row_max = lax.pmax(local_max, ("dp", "cent"))
    row_total = lax.psum(jnp.sum(jnp.exp(scores - row_max[:, None]), axis=1), ("dp", "cent"))
    log_total = row_max + jnp.log(row_total)
    probability = jnp.exp(scores - log_total[:, None])
    scale_up = centroids.shape[0] * lax.axis_size("dp") * lax.axis_size("cent") / gathered.shape[0]
    counts = scale_up * jnp.sum(probability, axis=0)
    prob_low = probability.astype(jnp.bfloat16)
    weighted = scale_up * lax.dot_general(
        prob_low, gathered, (((0,), (0,)), ((), ())), preferred_element_type=jnp.float32
    )
    return (weighted, counts)


def solution(mesh):
    in_specs = (
        P("dp", "cent"),
        P("dp", "cent"),
        P("cent", "dp"),
        P("cent"),
        P("cent", None),
        P(("dp", "cent"), None),
    )
    out_specs = (P(("dp", "cent"), None), P(("dp", "cent")))
    return jax.shard_map(body, mesh=mesh, in_specs=in_specs, out_specs=out_specs, check_vma=False)
```

profile of v0, /device:TPU:1, one launch (start us, length us, event | category | flops | bytes accessed | tf_op | source)
XLA Modules:
  0.0 617.1 jit_solution(13492038344672853306)
XLA Ops:
  7.2 0.0 copy-start
  7.2 0.0 copy-start.1
  7.2 0.0 copy-start.3
  7.2 0.0 copy-start.2
  7.2 0.0 all-gather.3.cloned.1.call-start
  7.3 0.7 all-gather.3.cloned.1.call-update
  7.9 0.0 reduce-scatter.2.cloned.1.call-start
  8.0 105.2 %all-gather.3.cloned.1.call-done = bf16[1376,4096]{1,0:T(8,128)(2,1)} async-done(((bf16[1376,128]{1,0:T(8,128)(2,1)}), bf16[1376,4096]{1,0:T(8,128)(2,1)}) %all-gather.3.cloned.1.call-update) | async-done | bytes 11272208 | tf_op jit(solution)/shard_map/all_gather | solution.py:11
  113.2 8.5 %fusion.11 = f32[176,4096]{1,0:T(8,128)} fusion(bf16[176,1376]{1,0:T(8,128)(2,1)} %param.6, bf16[1376,4096]{1,0:T(8,128)(2,1)} %all-gather.3.cloned.1.call-done), kind=kOutput, calls=%fused_computation.17 | convolution fusion | flops 1983905792 | bytes 14640128 | tf_op jit(solution)/shard_map/dot_general | solution.py:9
  121.7 0.0 reduce-scatter.2.cloned.1.call-update
  121.7 0.0 all-reduce.2.cloned.1.call-start
  121.8 103.8 %reduce-scatter.2.cloned.1.call-done = f32[176,512]{1,0:T(8,128)} async-done(((f32[176,4096]{1,0:T(8,128)}), f32[176,512]{1,0:T(8,128)}) %reduce-scatter.2.cloned.1.call-update) | async-done | bytes 360464 | tf_op jit(solution)/shard_map/reduce_scatter | solution.py:14
  225.6 0.0 copy-done.1
  225.6 0.0 copy-done.3
  225.6 0.0 copy-done.2
  225.6 2.2 fusion.8
  227.8 0.0 all-reduce.2.cloned.1.call-update
  227.8 0.0 all-gather.5.cloned.1.call-start
  227.8 112.2 %all-reduce.2.cloned.1.call-done = f32[176,1024]{1,0:T(8,128)} async-done(((f32[176,1024]{1,0:T(8,128)}), f32[176,1024]{1,0:T(8,128)}) %all-reduce.2.cloned.1.call-update) | async-done | bytes 720912 | tf_op jit(solution)/shard_map/psum | solution.py:18
  340.1 1.2 multiply_reduce_fusion
  341.3 2.0 multiply_convert_fusion
  343.3 0.0 all-gather.5.cloned.1.call-update
  343.3 78.9 %all-gather.5.cloned.1.call-done = bf16[5632,1024]{1,0:T(8,128)(2,1)} async-done(((bf16[176,1024]{1,0:T(8,128)(2,1)}), bf16[5632,1024]{1,0:T(8,128)(2,1)}) %all-gather.5.cloned.1.call-update) | async-done | bytes 11534352 | tf_op jit(solution)/shard_map/all_gather | solution.py:22
  422.2 0.0 copy-done
  422.2 13.2 %fusion.10 = (f32[5632]{0:T(1024)S(1)}, f32[5632,512]{0,1:T(8,128)}) fusion(bf16[5632,1024]{1,0:T(8,128)(2,1)} %all-gather.5.cloned.1.call-done, bf16[512,1024]{1,0:T(8,128)(2,1)S(1)} %copy-done), kind=kOutput, calls=%fused_computation.16 | convolution fusion | flops 5911341568 | bytes 24139776 | tf_op jit(solution)/shard_map/dot_general | solution.py:25
  435.3 76.1 %pmax.7 = f32[5632]{0:T(1024)S(1)} all-reduce(f32[5632]{0:T(1024)S(1)} %get-tuple-element.2), channel_id=1, replica_groups=mesh['dp'=32,'cent'=8] {'dp','cent'}, use_global_device_ids=true, to_apply=%region_4.0 | all-reduce | flops 5632 | bytes 45056 | tf_op jit(solution)/shard_map/pmax | solution.py:31
  511.4 6.0 exponential_reduce_fusion
  517.4 73.3 %psum.15 = f32[5632]{0:T(1024)S(1)} all-reduce(f32[5632]{0:T(1024)S(1)} %exponential_reduce_fusion), channel_id=1, replica_groups=mesh['dp'=32,'cent'=8] {'dp','cent'}, use_global_device_ids=true, to_apply=%region_6.0 | all-reduce | flops 5632 | bytes 45056 | tf_op jit(solution)/shard_map/psum | solution.py:32
  590.7 6.0 fusion
  596.7 0.6 broadcast_multiply_fusion
  597.3 13.3 %fusion.5 = f32[512,1024]{1,0:T(8,128)} fusion(bf16[5632,1024]{1,0:T(8,128)(2,1)} %all-gather.5.cloned.1.call-done, f32[5632,512]{0,1:T(8,128)} %get-tuple-element.3, f32[5632]{0:T(1024)S(1)} %log_add_fusion), kind=kOutput, calls=%fused_computation.7 | convolution fusion | flops 5911871488 | bytes 25188352 | tf_op jit(solution)/shard_map/dot_general | solution.py:38
  (2 shorter events, 0.0 us)
Async XLA Ops:
  7.2 415.0 %copy-start = (bf16[512,1024]{1,0:T(8,128)(2,1)S(1)}, bf16[512,1024]{1,0:T(8,128)(2,1)}, u32[]{:S(2)}) copy-start(bf16[512,1024]{1,0:T(8,128)(2,1)} %param.11) | copy-start | bytes 3145732
  7.2 218.4 %copy-start.1 = (bf16[512,1024]{1,0:T(8,128)(2,1)S(1)}, bf16[512,1024]{1,0:T(8,128)(2,1)}, u32[]{:S(2)}) copy-start(bf16[512,1024]{1,0:T(8,128)(2,1)} %param.10) | copy-start | bytes 3145732
  7.2 218.4 %copy-start.3 = (f32[512]{0:T(512)S(1)}, f32[512]{0:T(512)}, u32[]{:S(2)}) copy-start(f32[512]{0:T(512)} %param.9) | copy-start | bytes 6148
  7.2 218.4 %copy-start.2 = (bf16[176,512]{1,0:T(8,128)(2,1)S(1)}, bf16[176,512]{1,0:T(8,128)(2,1)}, u32[]{:S(2)}) copy-start(bf16[176,512]{1,0:T(8,128)(2,1)} %param.7) | copy-start | bytes 540676
  7.2 106.0 %all-gather.3.cloned.1.call-start = ((), (), s32[]{:S(2)}) async-start(), calls=%async_computation.1 | async-start | bytes 11624448 | tf_op jit(solution)/shard_map/all_gather | solution.py:11
  7.9 217.6 %reduce-scatter.2.cloned.1.call-start = ((), (), s32[]{:S(2)}) async-start(), calls=%async_computation.2 | async-start | bytes 3244032 | tf_op jit(solution)/shard_map/reduce_scatter | solution.py:14
  121.7 218.3 %all-reduce.2.cloned.1.call-start = ((), (), s32[]{:S(2)}) async-start(), calls=%async_computation.3 | async-start | bytes 1441792 | tf_op jit(solution)/shard_map/psum | solution.py:18
  227.8 194.4 %all-gather.5.cloned.1.call-start = ((), (), s32[]{:S(2)}) async-start(), calls=%async_computation.4 | async-start | bytes 11894784 | tf_op jit(solution)/shard_map/all_gather | solution.py:22
Sparse Core Ops, SparseCore 0:
  9.8 103.3 all-gather.2
  121.8 103.6 reduce-scatter.1
  228.8 111.2 all-reduce.1
  343.4 78.7 all-gather.4
where the time goes:
time: 618 us; the launch traced here: 617 us
  waiting for transfers between devices  401 us (65%)
  blocking collectives  149 us (24%)
  matrix products  37.1 us (6%)
  other arithmetic  15.8 us (3%)
  between operations  13.8 us (2%)
    psum x1, waiting for transfers between devices, body(): embed_full = lax.psum(partial_embed, 'cent')  112 us
    all_gather x1, waiting for transfers between devices, body(): lax.all_gather(down_weight, 'dp', axis=1, tiled=True)  105 us
    reduce_scatter x1, waiting for transfers between devices, body(): lax.psum_scatter(partial_layer, 'cent', scatter_dimension=1, tiled=True)  104 us
    all_gather x1, waiting for transfers between devices, body(): gathered = lax.all_gather(scaled, 'dp', axis=0, tiled=True)  78.9 us
    pmax x1, blocking collectives, body(): row_max = lax.pmax(local_max, ('dp', 'cent'))  76.1 us
    psum x1, blocking collectives, body(): lax.psum(jnp.sum(jnp.exp(scores - row_max[:, None]), axis=1), ('dp', 'cen...  73.3 us
    dot_general x1, matrix products, body(): lax.dot_general(prob_low, gathered, (((0,), (0,)), ((), ())), preferred_e...  13.3 us
    dot_general x1, matrix products, body(): lax.dot_general(gathered, centroids, (((1,), (1,)), ((), ())), preferred_...  13.2 us
  transfers between devices with their start and end apart: 4, of which 4 were waited for; matrix products, arithmetic and copies ran while one was open for 0% of the time, Pallas kernels for 0%

commit v1 on v0

--- a/solution.py
+++ b/solution.py
@@ -29,7 +29,9 @@
     )
     local_max = jnp.max(scores, axis=1)
     row_max = lax.pmax(local_max, ("dp", "cent"))
-    row_total = lax.psum(jnp.sum(jnp.exp(scores - row_max[:, None]), axis=1), ("dp", "cent"))
+    row_total = jnp.sum(
+        lax.all_gather(jnp.sum(jnp.exp(scores - row_max[:, None]), axis=1), ("dp", "cent")), axis=0
+    )
     log_total = row_max + jnp.log(row_total)
     probability = jnp.exp(scores - log_total[:, None])
     scale_up = centroids.shape[0] * lax.axis_size("dp") * lax.axis_size("cent") / gathered.shape[0]

time: 618 us -> 1270 us (2.06)
  waiting for transfers between devices: 401 us -> 1120 us
  blocking collectives: 149 us -> 76.3 us
    all_gather x0 -> x1, waiting for transfers between devices: none -> 715 us  [body(): lax.all_gather(jnp.sum(jnp.exp(scores - row_max[:, None]), axis=1), ('dp'...]
    psum x1 -> x0, blocking collectives: 73.3 us -> none  [body(): lax.psum(jnp.sum(jnp.exp(scores - row_max[:, None]), axis=1), ('dp', 'cen...]
  transfers between devices with their start and end apart: 4 -> 5, of which waited for: 4 -> 5; matrix products, arithmetic and copies ran while one was open for 0% -> 0% of each run, Pallas kernels for 0% -> 0%
where the time goes in v1:
time: 1270 us
  waiting for transfers between devices  1120 us (88%)
  blocking collectives  76.3 us (6%)
  matrix products  37.1 us (3%)
  other arithmetic  21.5 us (2%)
  between operations  13.8 us (1%)
    all_gather x1, waiting for transfers between devices, body(): lax.all_gather(jnp.sum(jnp.exp(scores - row_max[:, None]), axis=1), ('dp'...  715 us
    psum x1, waiting for transfers between devices, body(): embed_full = lax.psum(partial_embed, 'cent')  112 us
    all_gather x1, waiting for transfers between devices, body(): lax.all_gather(down_weight, 'dp', axis=1, tiled=True)  105 us
    reduce_scatter x1, waiting for transfers between devices, body(): lax.psum_scatter(partial_layer, 'cent', scatter_dimension=1, tiled=True)  104 us
    all_gather x1, waiting for transfers between devices, body(): gathered = lax.all_gather(scaled, 'dp', axis=0, tiled=True)  78.8 us
    pmax x1, blocking collectives, body(): row_max = lax.pmax(local_max, ('dp', 'cent'))  76.3 us
  transfers between devices with their start and end apart: 5, of which 5 were waited for; matrix products, arithmetic and copies ran while one was open for 0% of the time, Pallas kernels for 0%

profile of v1, /device:TPU:1, one launch (start us, length us, event | category | flops | bytes accessed | tf_op | source)
XLA Modules:
  0.0 1265.0 jit_solution(9648448004968659843)
XLA Ops:
  7.2 0.0 copy-start
  7.2 0.0 copy-start.1
  7.2 0.0 copy-start.3
  7.2 0.0 copy-start.2
  7.2 0.0 all-gather.6.cloned.1.call-start
  7.3 0.7 all-gather.6.cloned.1.call-update
  7.9 0.0 reduce-scatter.2.cloned.1.call-start
  8.0 105.2 %all-gather.6.cloned.1.call-done = bf16[1376,4096]{1,0:T(8,128)(2,1)} async-done(((bf16[1376,128]{1,0:T(8,128)(2,1)}), bf16[1376,4096]{1,0:T(8,128)(2,1)}) %all-gather.6.cloned.1.call-update) | async-done | bytes 11272208 | tf_op jit(solution)/shard_map/all_gather | solution.py:11
  113.2 8.5 fusion.11
  121.7 0.0 reduce-scatter.2.cloned.1.call-update
  121.7 0.0 all-reduce.2.cloned.1.call-start
  121.8 103.8 %reduce-scatter.2.cloned.1.call-done = f32[176,512]{1,0:T(8,128)} async-done(((f32[176,4096]{1,0:T(8,128)}), f32[176,512]{1,0:T(8,128)}) %reduce-scatter.2.cloned.1.call-update) | async-done | bytes 360464 | tf_op jit(solution)/shard_map/reduce_scatter | solution.py:14
  225.6 0.0 copy-done.1
  225.6 0.0 copy-done.3
  225.6 0.0 copy-done.2
  225.6 2.2 fusion.8
  227.8 0.0 all-reduce.2.cloned.1.call-update
  227.8 0.0 all-gather.8.cloned.1.call-start
  227.8 112.2 %all-reduce.2.cloned.1.call-done = f32[176,1024]{1,0:T(8,128)} async-done(((f32[176,1024]{1,0:T(8,128)}), f32[176,1024]{1,0:T(8,128)}) %all-reduce.2.cloned.1.call-update) | async-done | bytes 720912 | tf_op jit(solution)/shard_map/psum | solution.py:18
  340.1 1.2 multiply_reduce_fusion
  341.3 2.0 multiply_convert_fusion
  343.3 0.0 all-gather.8.cloned.1.call-update
  343.3 0.0 all-gather.10.cloned.1.call-start
  343.3 78.8 %all-gather.8.cloned.1.call-done = bf16[5632,1024]{1,0:T(8,128)(2,1)} async-done(((bf16[176,1024]{1,0:T(8,128)(2,1)}), bf16[5632,1024]{1,0:T(8,128)(2,1)}) %all-gather.8.cloned.1.call-update) | async-done | bytes 11534352 | tf_op jit(solution)/shard_map/all_gather | solution.py:22
  422.2 0.0 copy-done
  422.2 13.2 %fusion.10 = (f32[5632]{0:T(1024)S(1)}, f32[5632,512]{0,1:T(8,128)}) fusion(bf16[5632,1024]{1,0:T(8,128)(2,1)} %all-gather.8.cloned.1.call-done, bf16[512,1024]{1,0:T(8,128)(2,1)S(1)} %copy-done), kind=kOutput, calls=%fused_computation.16 | convolution fusion | flops 5911341568 | bytes 24139776 | tf_op jit(solution)/shard_map/dot_general | solution.py:25
  435.3 76.3 %pmax.7 = f32[5632]{0:T(1024)S(1)} all-reduce(f32[5632]{0:T(1024)S(1)} %get-tuple-element.2), channel_id=1, replica_groups=mesh['dp'=32,'cent'=8] {'dp','cent'}, use_global_device_ids=true, to_apply=%region_4.0 | all-reduce | flops 5632 | bytes 45056 | tf_op jit(solution)/shard_map/pmax | solution.py:31
  511.6 6.0 exponential_reduce_fusion
  517.6 0.6 reshape.16
  518.2 0.0 all-gather.10.cloned.1.call-update
  518.3 714.6 %all-gather.10.cloned.1.call-done = f32[256,1,5632]{2,1,0:T(1,128)} async-done(((f32[1,1,5632]{2,1,0:T(1,128)}), f32[256,1,5632]{2,1,0:T(1,128)}) %all-gather.10.cloned.1.call-update) | async-done | bytes 5767184 | tf_op jit(solution)/shard_map/all_gather | solution.py:33
  1232.9 5.7 reduce_sum.38
  1238.6 6.0 fusion
  1244.6 0.6 broadcast_multiply_fusion
  1245.2 13.3 %fusion.5 = f32[512,1024]{1,0:T(8,128)} fusion(bf16[5632,1024]{1,0:T(8,128)(2,1)} %all-gather.8.cloned.1.call-done, f32[5632,512]{0,1:T(8,128)} %get-tuple-element.3, f32[5632]{0:T(1024)S(1)} %log_add_fusion), kind=kOutput, calls=%fused_computation.7 | convolution fusion | flops 5911871488 | bytes 25188352 | tf_op jit(solution)/shard_map/dot_general | solution.py:40
  (2 shorter events, 0.0 us)
Async XLA Ops:
  7.2 415.0 %copy-start = (bf16[512,1024]{1,0:T(8,128)(2,1)S(1)}, bf16[512,1024]{1,0:T(8,128)(2,1)}, u32[]{:S(2)}) copy-start(bf16[512,1024]{1,0:T(8,128)(2,1)} %param.11) | copy-start | bytes 3145732
  7.2 218.4 %copy-start.1 = (bf16[512,1024]{1,0:T(8,128)(2,1)S(1)}, bf16[512,1024]{1,0:T(8,128)(2,1)}, u32[]{:S(2)}) copy-start(bf16[512,1024]{1,0:T(8,128)(2,1)} %param.10) | copy-start | bytes 3145732
  7.2 218.4 %copy-start.3 = (f32[512]{0:T(512)S(1)}, f32[512]{0:T(512)}, u32[]{:S(2)}) copy-start(f32[512]{0:T(512)} %param.9) | copy-start | bytes 6148
  7.2 218.4 %copy-start.2 = (bf16[176,512]{1,0:T(8,128)(2,1)S(1)}, bf16[176,512]{1,0:T(8,128)(2,1)}, u32[]{:S(2)}) copy-start(bf16[176,512]{1,0:T(8,128)(2,1)} %param.7) | copy-start | bytes 540676
  7.2 106.0 %all-gather.6.cloned.1.call-start = ((), (), s32[]{:S(2)}) async-start(), calls=%async_computation.1 | async-start | bytes 11624448 | tf_op jit(solution)/shard_map/all_gather | solution.py:11
  7.9 217.6 %reduce-scatter.2.cloned.1.call-start = ((), (), s32[]{:S(2)}) async-start(), calls=%async_computation.2 | async-start | bytes 3244032 | tf_op jit(solution)/shard_map/reduce_scatter | solution.py:14
  121.7 218.3 %all-reduce.2.cloned.1.call-start = ((), (), s32[]{:S(2)}) async-start(), calls=%async_computation.3 | async-start | bytes 1441792 | tf_op jit(solution)/shard_map/psum | solution.py:18
  227.8 194.4 %all-gather.8.cloned.1.call-start = ((), (), s32[]{:S(2)}) async-start(), calls=%async_computation.4 | async-start | bytes 11894784 | tf_op jit(solution)/shard_map/all_gather | solution.py:22
  343.3 889.6 %all-gather.10.cloned.1.call-start = ((), (), s32[]{:S(2)}) async-start(), calls=%async_computation.5 | async-start | bytes 5789696 | tf_op jit(solution)/shard_map/all_gather | solution.py:33
Sparse Core Ops, SparseCore 0:
  9.8 103.3 all-gather.5
  121.8 103.6 reduce-scatter.1
  228.8 111.2 all-reduce.1
  343.4 78.7 all-gather.7
  518.4 714.4 all-gather.9
